TPU v7x, 32 devices: a whole 2x2x4 slice. The times are simulated.
32 devices in a mesh: rep: 4 (over y, x), shard: 8 (over z, core).
Axes of the slice: x: 2, y: 2, z: 4, core: 2. Of those that a mesh axis runs over, the one named last changes fastest.
Arguments:
- tokens: bfloat16 [32, 512, 1024], P(('rep', 'shard')), may hold values from -6 to 6
- cotangent: bfloat16 [32, 512, 1024], P(('rep', 'shard')), may hold values from -6 to 6
- lengths: int32 [32], replicated, may hold values from 1 to 512, 12288 in all
- slot_sequence: int32 [32], P(('rep', 'shard')), may hold values from 0 to 31, each once
- step_count: int32 [1], replicated, may hold values from 1 to 20
- learn_rate: float32 [1], replicated, may hold values from 0.1 to 1
- attention_in: float32 [1024, 3, 1024], P('shard'), may hold values from -0.1875 to 0.1875
- attention_in_first: float32 [1024, 3, 1024], P('shard'), may hold values from -36 to 36
- attention_in_second: float32 [1024, 3, 1024], P('shard'), may hold values from 20 to 400
- attention_out: float32 [1024, 1024], P('shard'), may hold values from -1.5 to 1.5
- attention_out_first: float32 [1024, 1024], P('shard'), may hold values from -36 to 36
- attention_out_second: float32 [1024, 1024], P('shard'), may hold values from 20 to 400
- gate_up_weight: float32 [1024, 2, 2816], P('shard'), may hold values from -0.1875 to 0.1875
- gate_up_first: float32 [1024, 2, 2816], P('shard'), may hold values from -36 to 36
- gate_up_second: float32 [1024, 2, 2816], P('shard'), may hold values from 20 to 400
- down_weight: float32 [2816, 1024], P('shard'), may hold values from -0.109375 to 0.109375
- down_first: float32 [2816, 1024], P('shard'), may hold values from -36 to 36
- down_second: float32 [2816, 1024], P('shard'), may hold values from 20 to 400
Outputs:
- output: bfloat16 [32, 512, 1024], P(('rep', 'shard'))
- input_grad: float32 [32, 512, 1024], P(('rep', 'shard'))
- attention_in_grad: float32 [1024, 3, 1024], P('shard')
- attention_in_new: float32 [1024, 3, 1024], P('shard')
- attention_in_first_new: float32 [1024, 3, 1024], P('shard')
- attention_in_second_new: float32 [1024, 3, 1024], P('shard')
- attention_out_grad: float32 [1024, 1024], P('shard')
- attention_out_new: float32 [1024, 1024], P('shard')
- attention_out_first_new: float32 [1024, 1024], P('shard')
- attention_out_second_new: float32 [1024, 1024], P('shard')
- gate_up_grad: float32 [1024, 2, 2816], P('shard')
- gate_up_new: float32 [1024, 2, 2816], P('shard')
- gate_up_first_new: float32 [1024, 2, 2816], P('shard')
- gate_up_second_new: float32 [1024, 2, 2816], P('shard')
- down_grad: float32 [2816, 1024], P('shard')
- down_new: float32 [2816, 1024], P('shard')
- down_first_new: float32 [2816, 1024], P('shard')
- down_second_new: float32 [2816, 1024], P('shard')
Inputs may be any that keep to these rules, and one draw needn't show every extreme that they name: `lengths`: lengths of the sequences by number; they add up to 3 / 4 of 16384, and one is exactly 512. `slot_sequence`: A permutation of the 32 sequence numbers.
All inputs are finite; a program needn't handle non-finite values.
Results may differ from a plain program's by a relative error of at most 0.025.
The roundings to bfloat16 on the way count: a program that leaves them out, or rounds other values in their place, can miss the bound.
Values may be sent and summed in bfloat16 or wider, within the bound.
A program may use at most 256 MiB of HBM per device.

v0:
```python
import jax
import jax.numpy as jnp
from jax import lax
from jax.sharding import PartitionSpec as P

HD = 64
norm_eps = 1e-05
beta_first = 0.9
beta_second = 0.95
adam_eps = 1e-08
weight_decay = 0.1
rope_base = 10000.0
masked_score = -1e30


def layer_norm(values):
    centered = values - jnp.mean(values, axis=-1, keepdims=True)
    inverse = lax.rsqrt(jnp.mean(centered * centered, axis=-1, keepdims=True) + norm_eps)
    return (centered * inverse, inverse)


def norm_back(normed, inverse, upstream):
    mean_grad = jnp.mean(upstream, axis=-1, keepdims=True)
    mean_dot = jnp.mean(upstream * normed, axis=-1, keepdims=True)
    return inverse * (upstream - mean_grad - normed * mean_dot)


def rope_tables(position_count, head_size):
    half_size = head_size // 2
    frequency = rope_base ** (-(jnp.arange(half_size, dtype=jnp.float32) * 2.0 / head_size))
    angles = jnp.arange(position_count, dtype=jnp.float32)[:, None] * frequency[None, :]
    angles = jnp.concatenate([angles, angles], axis=1)
    return (jnp.cos(angles)[:, None, :], jnp.sin(angles)[:, None, :])


def rotate(values, cosine_table, sine_table):
    half_size = values.shape[-1] // 2
    turned = jnp.concatenate([-values[..., half_size:], values[..., :half_size]], axis=-1)
    return values * cosine_table + turned * sine_table


def masked_scores(queries, rotated_keys, length):
    position_count, head_size = (queries.shape[0], queries.shape[-1])
    scores = jnp.einsum(
        "qhd,khd->hqk", queries, rotated_keys, preferred_element_type=jnp.float32
    ) * head_size ** (-0.5)
    position = jnp.arange(position_count)
    allowed = (position[None, :] <= position[:, None]) & (position[None, :] < length)
    return jnp.where(allowed[None], scores, masked_score)


def attend_forward(pieces):
    queries, rotated_keys, values_low, length = pieces
    scores = masked_scores(queries, rotated_keys, length)
    row_max = jnp.max(scores, axis=-1, keepdims=True)
    exponent = jnp.exp(scores - row_max)
    row_sum = jnp.sum(exponent, axis=-1, keepdims=True)
    weights = (exponent / row_sum).astype(jnp.bfloat16)
    mixed_heads = jnp.einsum(
        "hqk,khd->qhd", weights, values_low, preferred_element_type=jnp.float32
    )
    return (mixed_heads, row_max + jnp.log(row_sum))


def attend_backward(pieces):
    queries, rotated_keys, values_low, length, log_total, mixed_grad = pieces
    head_size = queries.shape[-1]
    scores = masked_scores(queries, rotated_keys, length)
    probability = jnp.exp(scores - log_total)
    value_grad = jnp.einsum(
        "hqk,qhd->khd",
        probability.astype(jnp.bfloat16),
        mixed_grad,
        preferred_element_type=jnp.float32,
    )
    probability_grad = jnp.einsum(
        "qhd,khd->hqk", mixed_grad, values_low, preferred_element_type=jnp.float32
    )
    inner_dot = jnp.sum(probability * probability_grad, axis=-1, keepdims=True)
    score_grad = (probability * (probability_grad - inner_dot) * head_size ** (-0.5)).astype(
        jnp.bfloat16
    )
    query_grad = jnp.einsum(
        "hqk,khd->qhd", score_grad, rotated_keys, preferred_element_type=jnp.float32
    )
    key_grad = jnp.einsum("hqk,qhd->khd", score_grad, queries, preferred_element_type=jnp.float32)
    return (query_grad, key_grad, value_grad)


def adam_update(weight, first, second, gradient, step_count, learn_rate):
    steps_taken = step_count[0].astype(jnp.float32)
    first_new = beta_first * first + (1.0 - beta_first) * gradient
    second_new = beta_second * second + (1.0 - beta_second) * gradient * gradient
    first_hat = first_new / (1.0 - beta_first**steps_taken)
    second_hat = second_new / (1.0 - beta_second**steps_taken)
    weight_new = weight - learn_rate[0] * (
        first_hat / (jnp.sqrt(second_hat) + adam_eps) + weight_decay * weight
    )
    return (gradient, weight_new, first_new, second_new)


def gather_full(local, rep_count, rep_index):
    rows = local.shape[0]
    flat = local.reshape(rows, -1)
    width = flat.shape[1] // rep_count
    piece = lax.dynamic_slice_in_dim(flat, rep_index * width, width, axis=1)
    column = lax.all_gather(piece, "shard", axis=0, tiled=True)
    return lax.all_gather(column, "rep", axis=0, tiled=False)


def reduce_full(partial):
    part = lax.psum_scatter(partial, "rep", scatter_dimension=0, tiled=False)
    part = lax.psum_scatter(part, "shard", scatter_dimension=0, tiled=True)
    pieces = lax.all_gather(part, "rep", axis=0, tiled=False)
    rows = pieces.shape[1]
    return jnp.transpose(pieces, (1, 0, 2)).reshape(rows, -1).astype(jnp.float32)


def shards(
    tokens,
    cotangent,
    lengths,
    slot_sequence,
    step_count,
    learn_rate,
    attention_in,
    attention_in_first,
    attention_in_second,
    attention_out,
    attention_out_first,
    attention_out_second,
    gate_up_weight,
    gate_up_first,
    gate_up_second,
    down_weight,
    down_first,
    down_second,
):
    slot_count, position_count, feature_count = tokens.shape
    row_total = slot_count * position_count
    head_count = feature_count // HD
    shaped = (slot_count, position_count, head_count, HD)
    inputs = tokens.astype(jnp.float32).reshape(row_total, feature_count)
    matches = jnp.arange(lengths.shape[0])[None, :] == slot_sequence[:, None]
    slot_length = jnp.sum(jnp.where(matches, lengths[None, :], 0), axis=1)
    alive_rows = (
        (jnp.arange(position_count)[None, :] < slot_length[:, None])
        .astype(jnp.float32)
        .reshape(row_total, 1)
    )
    cosine_table, sine_table = rope_tables(position_count, HD)
    in_local = attention_in.astype(jnp.bfloat16)
    out_local = attention_out.astype(jnp.bfloat16)
    gate_up_local = gate_up_weight.astype(jnp.bfloat16)
    down_local = down_weight.astype(jnp.bfloat16)
    rep_count = lax.axis_size("rep")
    rep_index = lax.axis_index("rep")
    in_full = gather_full(in_local, rep_count, rep_index)
    out_full = gather_full(out_local, rep_count, rep_index)
    gate_up_full = gather_full(gate_up_local, rep_count, rep_index)
    down_full = gather_full(down_local, rep_count, rep_index)
    normed_one, inverse_one = layer_norm(inputs)
    first_input = normed_one.astype(jnp.bfloat16)
    projected = jnp.einsum(
        "rd,qde->rqe", first_input, in_full, preferred_element_type=jnp.float32
    ).reshape(row_total, 3, feature_count)
    queries = rotate(projected[:, 0].reshape(shaped), cosine_table, sine_table).astype(jnp.bfloat16)
    rotated_keys = rotate(projected[:, 1].reshape(shaped), cosine_table, sine_table).astype(
        jnp.bfloat16
    )
    values_low = projected[:, 2].reshape(shaped).astype(jnp.bfloat16)
    mixed_heads, log_total = lax.map(
        attend_forward, (queries, rotated_keys, values_low, slot_length)
    )
    mixed_low = mixed_heads.reshape(row_total, feature_count).astype(jnp.bfloat16)
    residual = inputs + jnp.einsum(
        "rd,qde->rqe", mixed_low, out_full, preferred_element_type=jnp.float32
    ).reshape(row_total, feature_count)
    normed_two, inverse_two = layer_norm(residual)
    second_input = normed_two.astype(jnp.bfloat16)
    gate_up = jnp.einsum(
        "rd,qdf->rqf", second_input, gate_up_full, preferred_element_type=jnp.float32
    ).reshape(row_total, 2, -1)
    gate_value = gate_up[:, 0]
    up_value = gate_up[:, 1]
    sigmoid_gate = jax.nn.sigmoid(gate_value)
    hidden_low = (gate_value * sigmoid_gate * up_value).astype(jnp.bfloat16)
    result = residual + jnp.einsum(
        "rf,qfe->rqe", hidden_low, down_full, preferred_element_type=jnp.float32
    ).reshape(row_total, feature_count)
    output = (result * alive_rows).astype(jnp.bfloat16).reshape(tokens.shape)
    output_grad = cotangent.astype(jnp.float32).reshape(row_total, feature_count) * alive_rows
    result_grad_low = output_grad.astype(jnp.bfloat16)
    hidden_grad = jnp.einsum(
        "rqe,qfe->rf",
        result_grad_low.reshape(row_total, rep_count, -1),
        down_full,
        preferred_element_type=jnp.float32,
    )
    gate_grad = hidden_grad * up_value * sigmoid_gate * (1.0 + gate_value * (1.0 - sigmoid_gate))
    up_grad = hidden_grad * gate_value * sigmoid_gate
    gate_up_grad_low = (
        jnp.concatenate([gate_grad, up_grad], axis=1)
        .astype(jnp.bfloat16)
        .reshape(row_total, rep_count, -1)
    )
    second_input_grad = jnp.einsum(
        "rqf,qdf->rd", gate_up_grad_low, gate_up_full, preferred_element_type=jnp.float32
    )
    residual_grad = output_grad + norm_back(normed_two, inverse_two, second_input_grad)
    down_part = reduce_full(
        jnp.einsum(
            "rc,rqe->qce",
            hidden_low,
            result_grad_low.reshape(row_total, rep_count, -1),
            preferred_element_type=jnp.float32,
        ).astype(jnp.bfloat16)
    )
    gate_up_part = reduce_full(
        jnp.einsum(
            "rc,rqf->qcf", second_input, gate_up_grad_low, preferred_element_type=jnp.float32
        ).astype(jnp.bfloat16)
    ).reshape(gate_up_weight.shape)
    branch_grad = residual_grad.astype(jnp.bfloat16)
    mixed_grad = (
        jnp.einsum(
            "rqe,qde->rd",
            branch_grad.reshape(row_total, rep_count, -1),
            out_full,
            preferred_element_type=jnp.float32,
        )
        .astype(jnp.bfloat16)
        .reshape(shaped)
    )
    query_grad, key_grad, value_grad = lax.map(
        attend_backward, (queries, rotated_keys, values_low, slot_length, log_total, mixed_grad)
    )
    query_back = rotate(query_grad, cosine_table, -sine_table).reshape(row_total, feature_count)
    key_back = rotate(key_grad, cosine_table, -sine_table).reshape(row_total, feature_count)
    projected_grad = (
        jnp.concatenate(
            [query_back, key_back, value_grad.reshape(row_total, feature_count)], axis=1
        )
        .astype(jnp.bfloat16)
        .reshape(row_total, rep_count, -1)
    )
    first_input_grad = jnp.einsum(
        "rqe,qde->rd", projected_grad, in_full, preferred_element_type=jnp.float32
    )
    input_grad = (residual_grad + norm_back(normed_one, inverse_one, first_input_grad)).reshape(
        tokens.shape
    )
    in_part = reduce_full(
        jnp.einsum(
            "rc,rqe->qce", first_input, projected_grad, preferred_element_type=jnp.float32
        ).astype(jnp.bfloat16)
    ).reshape(attention_in.shape)
    out_part = reduce_full(
        jnp.einsum(
            "rc,rqe->qce",
            mixed_low,
            branch_grad.reshape(row_total, rep_count, -1),
            preferred_element_type=jnp.float32,
        ).astype(jnp.bfloat16)
    )
    in_grad, in_new, in_first, in_second = adam_update(
        attention_in, attention_in_first, attention_in_second, in_part, step_count, learn_rate
    )
    out_grad, out_new, out_first, out_second = adam_update(
        attention_out, attention_out_first, attention_out_second, out_part, step_count, learn_rate
    )
    gu_grad, gu_new, gu_first, gu_second = adam_update(
        gate_up_weight, gate_up_first, gate_up_second, gate_up_part, step_count, learn_rate
    )
    dn_grad, dn_new, dn_first, dn_second = adam_update(
        down_weight, down_first, down_second, down_part, step_count, learn_rate
    )
    return (
        output,
        input_grad,
        in_grad,
        in_new,
        in_first,
        in_second,
        out_grad,
        out_new,
        out_first,
        out_second,
        gu_grad,
        gu_new,
        gu_first,
        gu_second,
        dn_grad,
        dn_new,
        dn_first,
        dn_second,
    )


def solution(mesh):
    return jax.shard_map(
        shards,
        mesh=mesh,
        in_specs=(
            P(("rep", "shard"), None, None),
            P(("rep", "shard"), None, None),
            P(),
            P(("rep", "shard")),
            P(),
            P(),
            P("shard", None, None),
            P("shard", None, None),
            P("shard", None, None),
            P("shard", None),
            P("shard", None),
            P("shard", None),
            P("shard", None, None),
            P("shard", None, None),
            P("shard", None, None),
            P("shard", None),
            P("shard", None),
            P("shard", None),
        ),
        out_specs=(
            P(("rep", "shard"), None, None),
            P(("rep", "shard"), None, None),
            P("shard", None, None),
            P("shard", None, None),
            P("shard", None, None),
            P("shard", None, None),
            P("shard", None),
            P("shard", None),
            P("shard", None),
            P("shard", None),
            P("shard", None, None),
            P("shard", None, None),
            P("shard", None, None),
            P("shard", None, None),
            P("shard", None),
            P("shard", None),
            P("shard", None),
            P("shard", None),
        ),
        check_vma=False,
    )
```

profile of v0, /device:TPU:0, one launch (start us, length us, event | category | flops | bytes accessed | tf_op | source)
XLA Modules:
  0.0 931.0 jit_solution(1859404770817627660)
XLA Ops:
  16.7 19.5 %all_gather.63 = bf16[1024,256]{1,0:T(8,128)(2,1)} all-gather(bf16[128,256]{1,0:T(8,128)(2,1)S(1)} %dynamic-slice_convert_fusion.1), channel_id=1, replica_groups=mesh['rep'=4,'shard'=8] {'shard'}, dimensions={0}, use_global_device_ids=true | all-gather | bytes 589824 | tf_op jit(solution)/shard_map/all_gather | solution.py:107
  43.8 37.6 %all-gather.19.cloned.1.call-done = bf16[1024,1408]{1,0:T(8,128)(2,1)} async-done(((bf16[128,1408]{1,0:T(8,128)(2,1)}), bf16[1024,1408]{1,0:T(8,128)(2,1)}) %all-gather.19.cloned.1.call-update) | async-done | bytes 2883600 | tf_op jit(solution)/shard_map/all_gather | solution.py:107
  88.0 18.9 %all-gather.21.cloned.1.call-done = bf16[2816,256]{1,0:T(8,128)(2,1)} async-done(((bf16[352,256]{1,0:T(8,128)(2,1)}), bf16[2816,256]{1,0:T(8,128)(2,1)}) %all-gather.21.cloned.1.call-update) | async-done | bytes 1441808 | tf_op jit(solution)/shard_map/all_gather | solution.py:107
  107.4 36.0 %all-gather.25.cloned.1.call-done = bf16[4096,256]{1,0:T(8,128)(2,1)} async-done(((bf16[1024,256]{1,0:T(8,128)(2,1)}), bf16[4096,256]{1,0:T(8,128)(2,1)}) %all-gather.25.cloned.1.call-update) | async-done | bytes 2097168 | tf_op jit(solution)/shard_map/all_gather | solution.py:108
  147.4 67.9 %all-gather.23.cloned.1.call-done = bf16[4096,768]{0,1:T(8,128)(2,1)} async-done(((bf16[1024,768]{0,1:T(8,128)(2,1)}), bf16[4096,768]{0,1:T(8,128)(2,1)}) %all-gather.23.cloned.1.call-update) | async-done | bytes 6291472 | tf_op jit(solution)/shard_map/all_gather | solution.py:108
  263.5 10.3 %fusion.4 = f32[16,512]{1,0:T(8,128)S(1)} fusion(f32[16,512,512]{1,2,0:T(8,128)} %get-tuple-element.181, f32[16,512]{1,0:T(8,128)S(1)} %get-tuple-element.180), kind=kLoop, calls=%fused_computation.8 | loop fusion | flops 8380416 | bytes 16842752 | tf_op jit(solution)/shard_map/while/body/eval_jaxpr/reduce_sum | solution.py:57
  284.8 46.0 %all-gather.27.cloned.1.call-done = bf16[4096,1408]{1,0:T(8,128)(2,1)} async-done(((bf16[1024,1408]{1,0:T(8,128)(2,1)}), bf16[4096,1408]{1,0:T(8,128)(2,1)}) %all-gather.27.cloned.1.call-update) | async-done | bytes 11534352 | tf_op jit(solution)/shard_map/all_gather | solution.py:108
  330.9 12.5 %fusion.79 = f32[512,4,1408]{0,2,1:T(8,128)} fusion(bf16[4,1024,1408]{2,1,0:T(8,128)(2,1)} %bitcast.296, f32[512,1024]{1,0:T(8,128)} %copy-done.7, f32[512]{0:T(512)S(1)} %add_rsqrt_fusion, f32[512]{0:T(512)S(1)} %broadcast_multiply_fusion.4), kind=kOutput, calls=%fused_computation.134 | convolution fusion | flops 5907152896 | bytes 25169920 | tf_op jit(solution)/shard_map/rd,qdf->rqf/dot_general | solution.py:181
  343.4 9.9 %fusion.97 = (f32[512,1,2816]{0,2,1:T(8,128)}, f32[512,1,2816]{0,2,1:T(8,128)}) fusion(f32[512,2,2816]{0,2,1:T(8,128)} %bitcast.256), kind=kLoop, calls=%fused_computation.157 | loop fusion | bytes 23068672 | tf_op jit(solution)/shard_map/slice | solution.py:184
  365.9 32.7 %all-gather.29.cloned.1.call-done = bf16[11264,256]{1,0:T(8,128)(2,1)} async-done(((bf16[2816,256]{1,0:T(8,128)(2,1)}), bf16[11264,256]{1,0:T(8,128)(2,1)}) %all-gather.29.cloned.1.call-update) | async-done | bytes 5767184 | tf_op jit(solution)/shard_map/all_gather | solution.py:108
  398.5 11.1 %fusion.25 = (bf16[512,2816]{1,0:T(8,128)(2,1)S(1)}, bf16[512,2816]{1,0:T(8,128)(2,1)S(1)}) fusion(f32[512,1,2816]{2,0,1:T(8,128)} %copy.240, f32[512,1,2816]{2,0,1:T(8,128)} %copy.241, bf16[4,2816,256]{2,1,0:T(8,128)(2,1)} %bitcast.263, f32[512,4,256]{2,1,0:T(4,128)} %reshape.396, f32[512]{0:T(512)S(1)} %fusion.87), kind=kOutput, calls=%fused_computation.30 | convolution fusion | flops 2972581888 | bytes 25167872 | tf_op jit(solution)/shard_map/rqe,qfe->rf/dot_general | solution.py:194
  414.0 11.1 %bitcast_reduce_fusion.1 = (f32[512]{0:T(512)S(1)}, f32[512]{0:T(512)S(1)}, f32[512,1024,1]{1,0,2:T(8,128)S(1)}) fusion(f32[512]{0:T(512)S(1)} %add_rsqrt_fusion, f32[512,1024]{1,0:T(8,128)S(1)} %copy-done.8, f32[512]{0:T(512)S(1)} %broadcast_multiply_fusion.4, bf16[512,4,1408]{2,0,1:T(8,128)(2,1)} %bitcast_dynamic-update-slice_fusion, ...), kind=kOutput, calls=%fused_computation.81 | convolution fusion | flops 5908200448 | bytes 21504000 | tf_op jit(solution)/shard_map/rqf,qdf->rd/dot_general | solution.py:207
  432.8 12.2 %fusion.6 = bf16[4,1024,1408]{1,2,0:T(8,128)(2,1)} fusion(bf16[512,4,1408]{2,0,1:T(8,128)(2,1)} %bitcast_dynamic-update-slice_fusion, f32[512,1024]{1,0:T(8,128)} %copy-done.7, f32[512]{0:T(512)S(1)} %add_rsqrt_fusion, f32[512]{0:T(512)S(1)} %broadcast_multiply_fusion.4), kind=kOutput, calls=%fused_computation.11 | convolution fusion | flops 5912920064 | bytes 19402752 | tf_op jit(solution)/shard_map/rc,rqf->qcf/dot_general | solution.py:220
  474.0 26.2 %fusion.16 = f32[16,64,512]{2,1,0:T(8,128)} fusion(bf16[512,16,64]{0,2,1:T(8,128)(2,1)} %copy-done.22, f32[16,512,512]{1,2,0:T(8,128)} %fusion.101, f32[16,512,512]{1,2,0:T(8,128)} %get-tuple-element.181, f32[16,512]{1,0:T(8,128)S(1)} %log_add_fusion), kind=kOutput, calls=%fused_computation.19 | convolution fusion | flops 566239744 | bytes 36732928 | tf_op jit(solution)/shard_map/while/body/eval_jaxpr/hqk,khd->qhd/dot_general | solution.py:83
  503.8 26.1 %fusion.13 = f32[16,64,512]{2,1,0:T(8,128)} fusion(bf16[512,16,64]{0,2,1:T(8,128)(2,1)S(1)} %copy-done.21, f32[16,512,512]{1,2,0:T(8,128)} %fusion.101, f32[16,512,512]{1,2,0:T(8,128)} %get-tuple-element.181, f32[16,512]{1,0:T(8,128)S(1)} %log_add_fusion), kind=kOutput, calls=%fused_computation.18 | convolution fusion | flops 566239744 | bytes 36732928 | tf_op jit(solution)/shard_map/while/body/eval_jaxpr/hqk,qhd->khd/dot_general | solution.py:86
  554.3 29.4 %reduce-scatter.37.cloned.1.call-done = bf16[1,1024,1408]{1,2,0:T(8,128)(2,1)} async-done(((bf16[4,1024,1408]{1,2,0:T(8,128)(2,1)}), bf16[1,1024,1408]{1,2,0:T(8,128)(2,1)}) %reduce-scatter.37.cloned.1.call-update) | async-done | bytes 2883600
  588.3 64.4 %reduce-scatter.39.cloned.1.call-done = bf16[1,2816,256]{1,2,0:T(8,128)(2,1)} async-done(((bf16[4,2816,256]{1,2,0:T(8,128)(2,1)}), bf16[1,2816,256]{1,2,0:T(8,128)(2,1)}) %reduce-scatter.39.cloned.1.call-update) | async-done | bytes 1441808
  655.2 70.9 %reduce-scatter.33.cloned.1.call-done = bf16[1,1024,768]{1,2,0:T(8,128)(2,1)} async-done(((bf16[4,1024,768]{1,2,0:T(8,128)(2,1)}), bf16[1,1024,768]{1,2,0:T(8,128)(2,1)}) %reduce-scatter.33.cloned.1.call-update) | async-done | bytes 1572880
  770.8 28.9 %reduce-scatter.29.cloned.1.call-done = bf16[128,1408]{1,0:T(8,128)(2,1)} async-done(((bf16[1024,1408]{1,0:T(8,128)(2,1)}), bf16[128,1408]{1,0:T(8,128)(2,1)}) %reduce-scatter.29.cloned.1.call-update) | async-done | bytes 360464
  803.1 32.4 %reduce-scatter.31.cloned.1.call-done = bf16[352,256]{1,0:T(8,128)(2,1)} async-done(((bf16[2816,256]{1,0:T(8,128)(2,1)}), bf16[352,256]{1,0:T(8,128)(2,1)}) %reduce-scatter.31.cloned.1.call-update) | async-done | bytes 180240 | tf_op jit(solution)/shard_map/reduce_scatter | solution.py:113
  835.5 11.4 %all-gather.7 = bf16[1408,256]{1,0:T(8,128)(2,1)S(1)} all-gather(bf16[352,256]{1,0:T(8,128)(2,1)} %reduce-scatter.31.cloned.1.call-done), channel_id=9, replica_groups=mesh['rep'=4,'shard'=8] {'rep'}, dimensions={0}, use_global_device_ids=true | all-gather | bytes 901120 | tf_op jit(solution)/shard_map/all_gather | solution.py:114
  852.6 18.0 %reduce-scatter.25.cloned.1.call-done = bf16[128,768]{1,0:T(8,128)(2,1)} async-done(((bf16[1024,768]{1,0:T(8,128)(2,1)}), bf16[128,768]{1,0:T(8,128)(2,1)}) %reduce-scatter.25.cloned.1.call-update) | async-done | bytes 196624 | tf_op jit(solution)/shard_map/reduce_scatter | solution.py:113
  870.7 15.6 %all-gather.4 = bf16[512,768]{1,0:T(8,128)(2,1)S(1)} all-gather(bf16[128,768]{1,0:T(8,128)(2,1)} %reduce-scatter.25.cloned.1.call-done), channel_id=6, replica_groups=mesh['rep'=4,'shard'=8] {'rep'}, dimensions={0}, use_global_device_ids=true | all-gather | bytes 983040 | tf_op jit(solution)/shard_map/all_gather | solution.py:114
  912.1 12.2 %multiply_subtract_fusion = (f32[128,2,2816]{2,1,0:T(2,128)}, f32[128,2,2816]{2,1,0:T(2,128)}, f32[128,2,2816]{2,1,0:T(2,128)}) fusion(f32[128,2,2816]{2,1,0:T(2,128)S(1)} %copy-done.3, f32[]{:T(128)} %bitcast.61, f32[]{:T(128)} %bitcast.60, f32[]{:T(128)} %bitcast.246, f32[128,2,2816]{2,1,0:T(2,128)} %reshape.404, f32[128,2,2816]{2,1,0:T(2,128)} %param.32, ...), kind=kLoop, calls=%fused_computation.45 | loop fusion | flops 10813440 | bytes 20185100 | tf_op jit(solution)/shard_map/sub | solution.py:96
  (218 shorter events, 252.8 us)
Async XLA Ops:
  7.2 36.6 %all-gather.17.cloned.1.call-start = ((), (), s32[]{:S(2)}) async-start(), calls=%async_computation.8 | async-start | bytes 1769472 | tf_op jit(solution)/shard_map/all_gather | solution.py:107
  10.1 71.3 %all-gather.19.cloned.1.call-start = ((), (), s32[]{:S(2)}) async-start(), calls=%async_computation.9 | async-start | bytes 3244032 | tf_op jit(solution)/shard_map/all_gather | solution.py:107
  14.0 92.9 %all-gather.21.cloned.1.call-start = ((), (), s32[]{:S(2)}) async-start(), calls=%async_computation.10 | async-start | bytes 1622016 | tf_op jit(solution)/shard_map/all_gather | solution.py:107
  15.7 127.7 %all-gather.25.cloned.1.call-start = ((), (), s32[]{:S(2)}) async-start(), calls=%async_computation.12 | async-start | bytes 2621440 | tf_op jit(solution)/shard_map/all_gather | solution.py:108
  36.2 179.1 %all-gather.23.cloned.1.call-start = ((), (), s32[]{:S(2)}) async-start(), calls=%async_computation.11 | async-start | bytes 7864320 | tf_op jit(solution)/shard_map/all_gather | solution.py:108
  43.7 38.5 %copy-start.4 = (bf16[1,512,1024]{2,1,0:T(8,128)(2,1)S(1)}, bf16[1,512,1024]{2,1,0:T(8,128)(2,1)}, u32[]{:S(2)}) copy-start(bf16[1,512,1024]{2,1,0:T(8,128)(2,1)} %param.19) | copy-start | bytes 3145732
  43.8 287.1 %all-gather.27.cloned.1.call-start = ((), (), s32[]{:S(2)}) async-start(), calls=%async_computation.13 | async-start | bytes 14417920 | tf_op jit(solution)/shard_map/all_gather | solution.py:108
  81.5 317.1 %all-gather.29.cloned.1.call-start = ((), (), s32[]{:S(2)}) async-start(), calls=%async_computation.14 | async-start | bytes 7208960 | tf_op jit(solution)/shard_map/all_gather | solution.py:108
  87.4 145.6 %copy-start.39 = (f32[512]{0:T(512)}, f32[512]{0:T(512)S(1)}, u32[]{:S(2)}) copy-start(f32[512]{0:T(512)S(1)} %broadcast_multiply_fusion.5) | copy-start | bytes 6148
  87.8 145.2 %copy-start.41 = (f32[512]{0:T(512)}, f32[512]{0:T(512)S(1)}, u32[]{:S(2)}) copy-start(f32[512]{0:T(512)S(1)} %add_rsqrt_fusion.1) | copy-start | bytes 6148
  106.9 445.2 %reduce-scatter.35.cloned.1.call-start = ((), (), s32[]{:S(2)}) async-start(), calls=%async_computation.21 | async-start | bytes 2621440
  432.7 150.9 %reduce-scatter.37.cloned.1.call-start = ((), (), s32[]{:S(2)}) async-start(), calls=%async_computation.22 | async-start | bytes 14417920
  445.0 207.7 %reduce-scatter.39.cloned.1.call-start = ((), (), s32[]{:S(2)}) async-start(), calls=%async_computation.23 | async-start | bytes 7208960
  458.7 267.4 %reduce-scatter.33.cloned.1.call-start = ((), (), s32[]{:S(2)}) async-start(), calls=%async_computation.20 | async-start | bytes 7864320
  503.7 28.1 %copy-start.33 = (f32[512,64]{0,1:T(8,128)S(1)}, f32[512,64]{0,1:T(8,128)}, u32[]{:S(2)}) copy-start(f32[512,64]{0,1:T(8,128)} %get-tuple-element.177) | copy-start | bytes 393220
  551.9 208.0 %reduce-scatter.27.cloned.1.call-start = ((), (), s32[]{:S(2)}) async-start(), calls=%async_computation.17 | async-start | bytes 589824
  554.2 245.5 %reduce-scatter.29.cloned.1.call-start = ((), (), s32[]{:S(2)}) async-start(), calls=%async_computation.18 | async-start | bytes 3244032
  588.2 247.3 %reduce-scatter.31.cloned.1.call-start = ((), (), s32[]{:S(2)}) async-start(), calls=%async_computation.19 | async-start | bytes 1622016 | tf_op jit(solution)/shard_map/reduce_scatter | solution.py:113
  655.2 215.5 %reduce-scatter.25.cloned.1.call-start = ((), (), s32[]{:S(2)}) async-start(), calls=%async_computation.16 | async-start | bytes 1769472 | tf_op jit(solution)/shard_map/reduce_scatter | solution.py:113
  728.7 172.1 %all-gather.31.cloned.1.call-start = ((), (), s32[]{:S(2)}) async-start(), calls=%async_computation.15 | async-start | bytes 1802240 | tf_op jit(solution)/shard_map/all_gather | solution.py:114
  760.8 40.9 %copy-start.32 = (f32[128,1024]{1,0:T(8,128)S(1)}, f32[128,1024]{1,0:T(8,128)}, u32[]{:S(2)}) copy-start(f32[128,1024]{1,0:T(8,128)} %param.27) | copy-start | bytes 1572868
  760.8 40.9 %copy-start.35 = (f32[128,1024]{1,0:T(8,128)S(1)}, f32[128,1024]{1,0:T(8,128)}, u32[]{:S(2)}) copy-start(f32[128,1024]{1,0:T(8,128)} %param.29) | copy-start | bytes 1572868
  760.9 40.9 %copy-start.36 = (f32[128,1024]{1,0:T(8,128)S(1)}, f32[128,1024]{1,0:T(8,128)}, u32[]{:S(2)}) copy-start(f32[128,1024]{1,0:T(8,128)} %param.28) | copy-start | bytes 1572868
  770.8 32.3 %copy-start.27 = (f32[16,8,4,256]{3,1,2,0:T(8,128)}, f32[16,8,4,256]{3,1,2,0:T(8,128)S(1)}, u32[]{:S(2)}) copy-start(f32[16,8,4,256]{3,1,2,0:T(8,128)S(1)} %copy.247) | copy-start | bytes 1572868
  (37 other events, 137.6 us)
Sparse Core Ops, SparseCore 0:
  10.3 33.4 all-gather.16
  46.0 35.4 all-gather.18
  83.6 23.2 all-gather.20
  108.6 34.8 all-gather.24
  145.1 70.1 all-gather.22
  217.0 113.7 all-gather.26
  332.7 65.7 all-gather.28
  432.9 35.1 reduce-scatter.34
  471.5 112.1 reduce-scatter.36
  586.8 65.8 reduce-scatter.38
  655.9 70.1 reduce-scatter.32
  728.9 30.9 reduce-scatter.26
  762.8 36.9 reduce-scatter.28
  802.5 32.9 reduce-scatter.30
  838.3 32.3 reduce-scatter.24
  872.9 27.8 all-gather.30
where the time goes:
time: 937 us; the launch traced here: 931 us
  waiting for transfers between devices  493 us (53%)
  matrix products  169 us (18%)
  local copies, waits for them, and re-layouts  134 us (14%)
  other arithmetic  61.3 us (7%)
  blocking collectives  55.9 us (6%)
  between operations  17 us (2%)
    unnamed x22, waiting for transfers between devices  195 us
    all_gather x4, waiting for transfers between devices, gather_full(): return lax.all_gather(column, 'rep', axis=0, tiled=False)  183 us
    all_gather x3, waiting for transfers between devices, gather_full(): column = lax.all_gather(piece, 'shard', axis=0, tiled=True)  64 us
    unnamed x108, local copies, waits for them, and re-layouts  59.1 us
    reduce_scatter x2, waiting for transfers between devices, reduce_full(): part = lax.psum_scatter(part, 'shard', scatter_dimension=0, tiled=True)  50.5 us
    all_gather x3, blocking collectives, reduce_full(): pieces = lax.all_gather(part, 'rep', axis=0, tiled=False)  36.4 us
    dot_general x1, matrix products, attend_backward(): jnp.einsum('hqk,khd->qhd', score_grad, rotated_keys, preferred_element_ty...  26.2 us
    dot_general x1, matrix products, attend_backward(): jnp.einsum('hqk,qhd->khd', score_grad, queries, preferred_element_type=jn...  26.1 us
  transfers between devices with their start and end apart: 16, of which 15 were waited for; matrix products, arithmetic and copies ran while one was open for 31% of the time, Pallas kernels for 0%

commit v1 on v0

--- a/solution.py
+++ b/solution.py
@@ -104,7 +104,14 @@
     flat = local.reshape(rows, -1)
     width = flat.shape[1] // rep_count
     piece = lax.dynamic_slice_in_dim(flat, rep_index * width, width, axis=1)
-    column = lax.all_gather(piece, "shard", axis=0, tiled=True)
+    ring = [piece]
+    for hop in range(7):
+        ring.append(lax.ppermute(ring[-1], "shard", [(dev, (dev + 1) % 8) for dev in range(8)]))
+    column = jnp.roll(
+        jnp.concatenate(ring[::-1], axis=0),
+        (lax.axis_index("shard") + 1) * ring[0].shape[0],
+        axis=0,
+    )
     return lax.all_gather(column, "rep", axis=0, tiled=False)
 
 

time: 937 us -> 884 us (0.943)
  waiting for transfers between devices: 493 us -> 449 us
  blocking collectives: 55.9 us -> 35.4 us
  local copies, waits for them, and re-layouts: 134 us -> 145 us
    ppermute x0 -> x28, waiting for transfers between devices: none -> 173 us  [gather_full(): lax.ppermute(ring[-1], 'shard', [(dev, (dev + 1) % 8) for dev in range(8)])]
    all_gather x4, waiting for transfers between devices: 183 us -> 29.7 us  [gather_full(): return lax.all_gather(column, 'rep', axis=0, tiled=False)]
    all_gather x3 -> x0, waiting for transfers between devices: 64 us -> none  [gather_full(): column = lax.all_gather(piece, 'shard', axis=0, tiled=True)]
    all_gather x1 -> x0, blocking collectives: 19.5 us -> none  [gather_full(): column = lax.all_gather(piece, 'shard', axis=0, tiled=True)]
    unnamed x108 -> x172, local copies, waits for them, and re-layouts: 59.1 us -> 61.9 us
    unnamed x22 -> x19, waiting for transfers between devices: 195 us -> 194 us
  transfers between devices with their start and end apart: 16 -> 41, of which waited for: 15 -> 34; matrix products, arithmetic and copies ran while one was open for 31% -> 34% of each run, Pallas kernels for 0% -> 0%
where the time goes in v1:
time: 884 us; the launch traced here: 875 us
  waiting for transfers between devices  449 us (51%)
  matrix products  169 us (19%)
  local copies, waits for them, and re-layouts  145 us (16%)
  other arithmetic  58.2 us (7%)
  blocking collectives  35.4 us (4%)
  between operations  17.4 us (2%)
    unnamed x19, waiting for transfers between devices  194 us
    ppermute x28, waiting for transfers between devices, gather_full(): lax.ppermute(ring[-1], 'shard', [(dev, (dev + 1) % 8) for dev in range(8)])  173 us
    unnamed x172, local copies, waits for them, and re-layouts  61.9 us
    reduce_scatter x2, waiting for transfers between devices, reduce_full(): part = lax.psum_scatter(part, 'shard', scatter_dimension=0, tiled=True)  52.1 us
    all_gather x3, blocking collectives, reduce_full(): pieces = lax.all_gather(part, 'rep', axis=0, tiled=False)  35.4 us
    all_gather x4, waiting for transfers between devices, gather_full(): return lax.all_gather(column, 'rep', axis=0, tiled=False)  29.7 us
    dot_general x1, matrix products, attend_backward(): jnp.einsum('hqk,khd->qhd', score_grad, rotated_keys, preferred_element_ty...  26.2 us
    dot_general x1, matrix products, attend_backward(): jnp.einsum('hqk,qhd->khd', score_grad, queries, preferred_element_type=jn...  26.1 us
  transfers between devices with their start and end apart: 41, of which 34 were waited for; matrix products, arithmetic and copies ran while one was open for 34% of the time, Pallas kernels for 0%

profile of v1, /device:TPU:0, one launch (start us, length us, event | category | flops | bytes accessed | tf_op | source)
XLA Modules:
  0.0 875.5 jit_solution(2867055553626123410)
XLA Ops:
  98.6 8.6 collective-permute-done.15
  107.2 8.6 collective-permute-done.16
  115.9 8.6 collective-permute-done.17
  124.5 8.6 collective-permute-done.18
  133.2 8.6 collective-permute-done.19
  209.6 8.7 copy.182
  276.9 12.5 %fusion.79 = f32[512,4,1408]{0,2,1:T(8,128)} fusion(bf16[4,1024,1408]{2,1,0:T(8,128)(2,1)} %bitcast.300, f32[512,1024]{1,0:T(8,128)} %copy-done.8, f32[512]{0:T(512)S(1)} %add_rsqrt_fusion, f32[512]{0:T(512)S(1)} %broadcast_multiply_fusion.4), kind=kOutput, calls=%fused_computation.198 | convolution fusion | flops 5907152896 | bytes 25169920 | tf_op jit(solution)/shard_map/rd,qdf->rqf/dot_general | solution.py:188
  289.4 9.9 %fusion.97 = (f32[512,1,2816]{0,2,1:T(8,128)}, f32[512,1,2816]{0,2,1:T(8,128)}) fusion(f32[512,2,2816]{0,2,1:T(8,128)} %bitcast.256), kind=kLoop, calls=%fused_computation.225 | loop fusion | bytes 23068672 | tf_op jit(solution)/shard_map/slice | solution.py:191
  312.3 29.7 %all-gather.20.cloned.1.call-done = bf16[11264,256]{1,0:T(8,128)(2,1)} async-done(((bf16[2816,256]{1,0:T(8,128)(2,1)}), bf16[11264,256]{1,0:T(8,128)(2,1)}) %all-gather.20.cloned.1.call-update) | async-done | bytes 5767184 | tf_op jit(solution)/shard_map/all_gather | solution.py:115
  342.0 11.1 %fusion.25 = (bf16[512,2816]{1,0:T(8,128)(2,1)S(1)}, bf16[512,2816]{1,0:T(8,128)(2,1)S(1)}) fusion(f32[512,1,2816]{2,0,1:T(8,128)} %copy.240, f32[512,1,2816]{2,0,1:T(8,128)} %copy.241, bf16[4,2816,256]{2,1,0:T(8,128)(2,1)} %bitcast.263, f32[512,4,256]{2,1,0:T(4,128)} %reshape.396, f32[512]{0:T(512)S(1)} %get-tuple-element.189), kind=kOutput, calls=%fused_computation.30 | convolution fusion | flops 2972581888 | bytes 25167872 | tf_op jit(solution)/shard_map/rqe,qfe->rf/dot_general | solution.py:201
  357.5 11.1 %bitcast_reduce_fusion.1 = (f32[512]{0:T(512)S(1)}, f32[512]{0:T(512)S(1)}, f32[512,1024,1]{1,0,2:T(8,128)S(1)}) fusion(f32[512]{0:T(512)S(1)} %add_rsqrt_fusion, f32[512,1024]{1,0:T(8,128)S(1)} %copy-done.9, f32[512]{0:T(512)S(1)} %broadcast_multiply_fusion.4, bf16[512,4,1408]{2,0,1:T(8,128)(2,1)} %bitcast_dynamic-update-slice_fusion, ...), kind=kOutput, calls=%fused_computation.81 | convolution fusion | flops 5908200448 | bytes 21504000 | tf_op jit(solution)/shard_map/rqf,qdf->rd/dot_general | solution.py:214
  376.3 12.1 %fusion.6 = bf16[4,1024,1408]{1,2,0:T(8,128)(2,1)} fusion(bf16[512,4,1408]{2,0,1:T(8,128)(2,1)} %bitcast_dynamic-update-slice_fusion, f32[512,1024]{1,0:T(8,128)} %copy-done.8, f32[512]{0:T(512)S(1)} %add_rsqrt_fusion, f32[512]{0:T(512)S(1)} %broadcast_multiply_fusion.4), kind=kOutput, calls=%fused_computation.11 | convolution fusion | flops 5912920064 | bytes 19402752 | tf_op jit(solution)/shard_map/rc,rqf->qcf/dot_general | solution.py:227
  417.5 26.2 %fusion.16 = f32[16,64,512]{2,1,0:T(8,128)} fusion(bf16[512,16,64]{0,2,1:T(8,128)(2,1)} %copy-done.23, f32[16,512,512]{1,2,0:T(8,128)} %fusion.101, f32[16,512,512]{1,2,0:T(8,128)} %get-tuple-element.181, f32[16,512]{1,0:T(8,128)S(1)} %log_add_fusion), kind=kOutput, calls=%fused_computation.19 | convolution fusion | flops 566239744 | bytes 36732928 | tf_op jit(solution)/shard_map/while/body/eval_jaxpr/hqk,khd->qhd/dot_general | solution.py:83
  447.3 26.1 %fusion.13 = f32[16,64,512]{2,1,0:T(8,128)} fusion(bf16[512,16,64]{0,2,1:T(8,128)(2,1)S(1)} %copy-done.22, f32[16,512,512]{1,2,0:T(8,128)} %fusion.101, f32[16,512,512]{1,2,0:T(8,128)} %get-tuple-element.181, f32[16,512]{1,0:T(8,128)S(1)} %log_add_fusion), kind=kOutput, calls=%fused_computation.18 | convolution fusion | flops 566239744 | bytes 36732928 | tf_op jit(solution)/shard_map/while/body/eval_jaxpr/hqk,qhd->khd/dot_general | solution.py:86
  497.8 29.2 %reduce-scatter.37.cloned.1.call-done = bf16[1,1024,1408]{1,2,0:T(8,128)(2,1)} async-done(((bf16[4,1024,1408]{1,2,0:T(8,128)(2,1)}), bf16[1,1024,1408]{1,2,0:T(8,128)(2,1)}) %reduce-scatter.37.cloned.1.call-update) | async-done | bytes 2883600
  531.6 64.5 %reduce-scatter.39.cloned.1.call-done = bf16[1,2816,256]{1,2,0:T(8,128)(2,1)} async-done(((bf16[4,2816,256]{1,2,0:T(8,128)(2,1)}), bf16[1,2816,256]{1,2,0:T(8,128)(2,1)}) %reduce-scatter.39.cloned.1.call-update) | async-done | bytes 1441808
  598.7 70.9 %reduce-scatter.33.cloned.1.call-done = bf16[1,1024,768]{1,2,0:T(8,128)(2,1)} async-done(((bf16[4,1024,768]{1,2,0:T(8,128)(2,1)}), bf16[1,1024,768]{1,2,0:T(8,128)(2,1)}) %reduce-scatter.33.cloned.1.call-update) | async-done | bytes 1572880
  704.4 9.3 %all-gather.5 = bf16[512,256]{0,1:T(8,128)(2,1)S(1)} all-gather(bf16[128,256]{0,1:T(8,128)(2,1)S(1)} %copy.235), channel_id=7, replica_groups=mesh['rep'=4,'shard'=8] {'rep'}, dimensions={0}, use_global_device_ids=true | all-gather | bytes 327680 | tf_op jit(solution)/shard_map/all_gather | solution.py:121
  714.3 28.9 %reduce-scatter.29.cloned.1.call-done = bf16[128,1408]{1,0:T(8,128)(2,1)} async-done(((bf16[1024,1408]{1,0:T(8,128)(2,1)}), bf16[128,1408]{1,0:T(8,128)(2,1)}) %reduce-scatter.29.cloned.1.call-update) | async-done | bytes 360464
  746.6 32.6 %reduce-scatter.31.cloned.1.call-done = bf16[352,256]{1,0:T(8,128)(2,1)} async-done(((bf16[2816,256]{1,0:T(8,128)(2,1)}), bf16[352,256]{1,0:T(8,128)(2,1)}) %reduce-scatter.31.cloned.1.call-update) | async-done | bytes 180240 | tf_op jit(solution)/shard_map/reduce_scatter | solution.py:120
  779.2 11.4 %all-gather.7 = bf16[1408,256]{1,0:T(8,128)(2,1)S(1)} all-gather(bf16[352,256]{1,0:T(8,128)(2,1)} %reduce-scatter.31.cloned.1.call-done), channel_id=9, replica_groups=mesh['rep'=4,'shard'=8] {'rep'}, dimensions={0}, use_global_device_ids=true | all-gather | bytes 901120 | tf_op jit(solution)/shard_map/all_gather | solution.py:121
  794.8 19.5 %reduce-scatter.25.cloned.1.call-done = bf16[128,768]{1,0:T(8,128)(2,1)} async-done(((bf16[1024,768]{1,0:T(8,128)(2,1)}), bf16[128,768]{1,0:T(8,128)(2,1)}) %reduce-scatter.25.cloned.1.call-update) | async-done | bytes 196624 | tf_op jit(solution)/shard_map/reduce_scatter | solution.py:120
  814.3 14.7 %all-gather.4 = bf16[512,768]{1,0:T(8,128)(2,1)S(1)} all-gather(bf16[128,768]{1,0:T(8,128)(2,1)} %reduce-scatter.25.cloned.1.call-done), channel_id=6, replica_groups=mesh['rep'=4,'shard'=8] {'rep'}, dimensions={0}, use_global_device_ids=true | all-gather | bytes 983040 | tf_op jit(solution)/shard_map/all_gather | solution.py:121
  856.5 12.2 %multiply_subtract_fusion = (f32[128,2,2816]{2,1,0:T(2,128)}, f32[128,2,2816]{2,1,0:T(2,128)}, f32[128,2,2816]{2,1,0:T(2,128)}) fusion(f32[128,2,2816]{2,1,0:T(2,128)S(1)} %copy-done.4, f32[]{:T(128)} %bitcast.61, f32[]{:T(128)} %bitcast.60, f32[]{:T(128)} %bitcast.246, f32[128,2,2816]{2,1,0:T(2,128)} %reshape.404, f32[128,2,2816]{2,1,0:T(2,128)} %param.32, ...), kind=kLoop, calls=%fused_computation.45 | loop fusion | flops 10813440 | bytes 20185100 | tf_op jit(solution)/shard_map/sub | solution.py:96
  (335 shorter events, 374.2 us)
Async XLA Ops:
  7.2 198.4 %all-gather.16.cloned.1.call-start = ((), (), s32[]{:S(2)}) async-start(), calls=%async_computation.9 | async-start | bytes 2621440 | tf_op jit(solution)/shard_map/all_gather | solution.py:115
  25.6 16.5 %collective-permute-start = (bf16[128,768]{0,1:T(8,128)(2,1)S(1)}, bf16[128,768]{0,1:T(8,128)(2,1)S(1)}, u32[]{:S(2)}, u32[]{:S(2)}) collective-permute-start(bf16[128,768]{0,1:T(8,128)(2,1)S(1)} %constant_dynamic-slice_fusion.5), channel_id=1, source_target_pairs={{0,1},{1,2},{2,3},{3,4},{4,5},{5,6},{6,7},{7,0},{8,9},{9,10},{10,1... | collective-permute-start | bytes 589832 | tf_op jit(solution)/shard_map/ppermute | solution.py:109
  42.1 8.4 collective-permute-start.1
  50.5 159.1 %all-gather.14.cloned.1.call-start = ((), (), s32[]{:S(2)}) async-start(), calls=%async_computation.8 | async-start | bytes 7864320 | tf_op jit(solution)/shard_map/all_gather | solution.py:115
  50.5 6.9 collective-permute-start.2
  57.5 6.9 collective-permute-start.3
  88.6 188.3 %all-gather.18.cloned.1.call-start = ((), (), s32[]{:S(2)}) async-start(), calls=%async_computation.10 | async-start | bytes 14417920 | tf_op jit(solution)/shard_map/all_gather | solution.py:115
  89.9 8.7 collective-permute-start.14
  98.6 8.6 collective-permute-start.15
  107.2 8.6 collective-permute-start.16
  115.9 8.6 collective-permute-start.17
  124.5 8.6 collective-permute-start.18
  133.2 8.6 collective-permute-start.19
  141.8 8.6 collective-permute-start.20
  153.0 189.0 %all-gather.20.cloned.1.call-start = ((), (), s32[]{:S(2)}) async-start(), calls=%async_computation.11 | async-start | bytes 7208960 | tf_op jit(solution)/shard_map/all_gather | solution.py:115
  205.1 290.6 %reduce-scatter.35.cloned.1.call-start = ((), (), s32[]{:S(2)}) async-start(), calls=%async_computation.18 | async-start | bytes 2621440
  376.2 150.8 %reduce-scatter.37.cloned.1.call-start = ((), (), s32[]{:S(2)}) async-start(), calls=%async_computation.19 | async-start | bytes 14417920
  388.4 207.7 %reduce-scatter.39.cloned.1.call-start = ((), (), s32[]{:S(2)}) async-start(), calls=%async_computation.20 | async-start | bytes 7208960
  402.1 267.4 %reduce-scatter.33.cloned.1.call-start = ((), (), s32[]{:S(2)}) async-start(), calls=%async_computation.17 | async-start | bytes 7864320
  495.5 208.0 %reduce-scatter.27.cloned.1.call-start = ((), (), s32[]{:S(2)}) async-start(), calls=%async_computation.14 | async-start | bytes 589824
  497.8 245.4 %reduce-scatter.29.cloned.1.call-start = ((), (), s32[]{:S(2)}) async-start(), calls=%async_computation.15 | async-start | bytes 3244032
  531.6 247.6 %reduce-scatter.31.cloned.1.call-start = ((), (), s32[]{:S(2)}) async-start(), calls=%async_computation.16 | async-start | bytes 1622016 | tf_op jit(solution)/shard_map/reduce_scatter | solution.py:120
  598.6 215.7 %reduce-scatter.25.cloned.1.call-start = ((), (), s32[]{:S(2)}) async-start(), calls=%async_computation.13 | async-start | bytes 1769472 | tf_op jit(solution)/shard_map/reduce_scatter | solution.py:120
  672.2 173.0 %all-gather.22.cloned.1.call-start = ((), (), s32[]{:S(2)}) async-start(), calls=%async_computation.12 | async-start | bytes 1802240 | tf_op jit(solution)/shard_map/all_gather | solution.py:121
  (64 other events, 742.5 us)
Sparse Core Ops, SparseCore 0:
  50.6 34.0 all-gather.15
  88.7 68.8 all-gather.13
  160.1 113.7 all-gather.17
  276.2 65.7 all-gather.19
  376.3 35.1 reduce-scatter.34
  414.8 112.1 reduce-scatter.36
  530.3 65.7 reduce-scatter.38
  599.3 70.1 reduce-scatter.32
  672.5 30.9 reduce-scatter.26
  706.2 36.9 reduce-scatter.28
  746.1 33.0 reduce-scatter.30
  781.9 32.3 reduce-scatter.24
  816.7 27.8 all-gather.21
